TPU v7x, 32 devices: a whole 2x2x4 slice. The times are simulated.
32 devices in a mesh: group: 2 (over y), chan: 4 (over z), band: 2 (over x), beam: 2 (over core).
Axes of the slice: x: 2, y: 2, z: 4, core: 2. Of those that a mesh axis runs over, the one named last changes fastest.
Arguments:
- voltages: bfloat16 [2, 1024, 2, 8, 512], P(None, 'chan', 'band', None, 'group'), parts along dimension 4, may hold values from -6 to 6
- gains: float32 [2, 2, 8, 1024], P(None, 'band', 'chan'), may hold values from -5 to 5
- positions: float32 [3, 1024], replicated, may hold values from -4 to 4
- directions: float32 [3, 2048], P(None, ('group', 'beam')), parts along dimension 1, may hold values from -1 to 1
- antenna_row_lookup: int32 [1024], replicated, may hold values from 0 to 1023, each once
- chan_order: int32 [16], replicated, may hold values from 0 to 15, each once
- delays: int32 [4, 2, 8], replicated, may hold values from 0 to 31
Outputs:
- dedispersed: float32 [2, 8, 32, 2048], P('band', 'chan', None, ('group', 'beam')), parts along dimension 3
There are 2 independent parts, one for each index of `group`. A program takes and returns all parts, laid end to end along the dimension named above; an argument that names none is the same for every part. Nothing has to cross between parts.
Inputs may be any that keep to these rules, and one draw needn't show every extreme that they name: `antenna_row_lookup`: each antenna appears once. `chan_order`: each frequency index appears once.
All inputs are finite; a program needn't handle non-finite values.
Results may differ from a plain program's by a relative error of at most 0.004.
Values may be sent and summed in bfloat16 or wider, within the bound.
A program may use at most 64 MiB of HBM per device.

v0:
```python
import math
import jax
import jax.numpy as jnp
from jax import lax
from jax.sharding import PartitionSpec as P

INTEG = 8


def partner_2(value, axis, distance):
    mask = 2**distance
    pairs = [(source, source ^ mask) for source in range(lax.axis_size(axis))]
    return lax.ppermute(value, axis, pairs)


def roll_rows(state, shifts):
    length = state.shape[1]
    doubled = jnp.concatenate([state, state], axis=1)

    def one_row(row, shift):
        return lax.dynamic_slice_in_dim(row, length - shift, length, 0)

    return jax.vmap(one_row)(doubled, shifts)


def pair_round(state, shifts, stride):
    count, length, width = state.shape
    grouped = state.reshape(count // (2 * stride), 2, stride, length, width)
    lower = jnp.broadcast_to(grouped[:, 0:1], grouped.shape).reshape(state.shape)
    upper = jnp.broadcast_to(grouped[:, 1:2], grouped.shape).reshape(state.shape)
    return lower + roll_rows(upper, shifts)


def partner_round(state, partner, upper_side, shifts):
    lower = jnp.where(upper_side, partner, state)
    upper = jnp.where(upper_side, state, partner)
    return lower + roll_rows(upper, shifts)


def beam_weights(gain_pair, freq, pos_rows, dirs):
    geometry = pos_rows[0][:, None] * dirs[0][None, :]
    geometry = geometry + pos_rows[1][:, None] * dirs[1][None, :]
    geometry = geometry + pos_rows[2][:, None] * dirs[2][None, :]
    phase = (2.0 * math.pi * freq)[:, None, None] * geometry[None]
    cosine = jnp.cos(phase)
    sine = jnp.sin(phase)
    g_re = gain_pair[0][:, :, None]
    g_im = gain_pair[1][:, :, None]
    factor = 1.0 / math.sqrt(pos_rows.shape[1])
    w_re = ((g_re * cosine + g_im * sine) * factor).astype(jnp.bfloat16)
    w_im = ((g_im * cosine - g_re * sine) * factor).astype(jnp.bfloat16)
    upper_rows = jnp.concatenate([w_re, w_im], axis=2)
    lower_rows = jnp.concatenate([-w_im, w_re], axis=2)
    return jnp.stack([upper_rows, lower_rows], axis=1)


def integrate(power, chans):
    count, samples, width = power.shape
    binned = jnp.mean(power.reshape(count, samples // INTEG, INTEG, width), axis=2)
    centred = binned - jnp.mean(binned, axis=1, keepdims=True)
    return centred * (1.0 / math.sqrt(chans))


def shards(voltages, gains, positions, directions, antenna_row_lookup, chan_order, delays):
    chan_count = lax.axis_size("chan")
    band_count = lax.axis_size("band")
    per_dev = gains.shape[2]
    in_band = per_dev * chan_count
    total = in_band * band_count
    chan_index = lax.axis_index("chan")
    band_index = lax.axis_index("band")
    base = band_index * in_band + chan_index * per_dev
    freq = 1.0 + lax.dynamic_slice_in_dim(chan_order, base, per_dev).astype(jnp.float32) / total
    pos_rows = positions[:, antenna_row_lookup]
    weights = beam_weights(gains[:, 0], freq, pos_rows, directions)
    turned = lax.all_to_all(voltages, "chan", split_axis=3, concat_axis=1, tiled=True)
    flat = turned.reshape(turned.shape[0], turned.shape[1], turned.shape[3], turned.shape[4])
    beams = jnp.einsum("pacn,cpaq->cnq", flat, weights, preferred_element_type=jnp.float32)
    half = beams.shape[2] // 2
    power = beams[:, :, :half] * beams[:, :, :half] + beams[:, :, half:] * beams[:, :, half:]
    state = integrate(power, total)
    flat_delays = delays.reshape(delays.shape[0], total)
    local_bits = per_dev.bit_length() - 1
    chan_bits = chan_count.bit_length() - 1
    band_bits = band_count.bit_length() - 1
    bit = 0
    shifts = lax.dynamic_slice_in_dim(flat_delays[bit], base, per_dev)
    state = pair_round(state, shifts, 1 << bit)
    for bit in range(chan_bits):
        level_no = local_bits + bit
        shifts = lax.dynamic_slice_in_dim(flat_delays[level_no], base, per_dev)
        partner = partner_2(state, "chan", bit)
        upper_side = chan_index // (1 << bit) % 2 == 1
        state = partner_round(state, partner, upper_side, shifts)
    for bit in range(band_bits):
        level_no = local_bits + chan_bits + bit
        shifts = lax.dynamic_slice_in_dim(flat_delays[level_no], base, per_dev)
        partner = partner_2(state, "band", bit)
        upper_side = band_index // (1 << bit) % 2 == 1
        state = partner_round(state, partner, upper_side, shifts)
    return state.reshape(1, per_dev, state.shape[1], state.shape[2])


def solution(mesh):
    placed = (
        P(None, "chan", "band", None, "group"),
        P(None, "band", "chan", None),
        P(),
        P(None, ("group", "beam")),
        P(),
        P(),
        P(),
    )
    return jax.shard_map(
        shards,
        mesh=mesh,
        in_specs=placed,
        out_specs=P("band", "chan", None, ("group", "beam")),
        check_vma=False,
    )
```

profile of v0, /device:TPU:0, one launch (start us, length us, event | category | flops | bytes accessed | tf_op | source)
XLA Modules:
  0.0 94.2 jit_solution(8014257760844754673)
XLA Ops:
  0.0 3.5 %copy.29 = bf16[2,256,1,8,256]{4,1,2,0,3:T(8,128)(2,1)} copy(bf16[2,256,1,8,256]{4,3,2,1,0:T(8,128)(2,1)} %param.7) | data formatting | bytes 4194304 | tf_op args[0]
  3.5 6.4 %all-to-all-start = ((bf16[2,256,1,8,256]{4,1,2,0,3:T(8,128)(2,1)}), bf16[2,256,1,8,256]{4,1,2,0,3:T(8,128)(2,1)S(1)}, u32[]{:S(2)}, u32[]{:S(2)}) async-start(bf16[2,256,1,8,256]{4,1,2,0,3:T(8,128)(2,1)} %copy.29), calls=%async_computation | async-start | bytes 4194304 | tf_op jit(solution)/shard_map/all_to_all | solution.py:76
  9.9 0.2 copy.27
  10.3 2.8 %gather_fusion = f32[1024,3]{1,0:T(8,128)S(1)} fusion(f32[3,1024]{0,1:T(8,128)S(1)} %copy.27, s32[1024]{0:T(1024)S(1)} %fusion.21), kind=kCustom, calls=%fused_computation | custom fusion | bytes 28672 | tf_op jit(solution)/shard_map/gather | solution.py:74
  13.3 0.8 slice_reduce_fusion.2
  14.1 0.5 multiply_add_fusion
  14.6 15.9 %fusion.10 = bf16[2,1024,512]{2,1,0:T(8,128)(2,1)S(1)} fusion(f32[2,1024]{1,0:T(2,128)S(1)} %get-tuple-element.15, f32[1024,512]{1,0:T(8,128)S(1)} %multiply_add_fusion, f32[2]{0:T(128)S(1)} %add_multiply_fusion, f32[2,1024]{1,0:T(2,128)S(1)} %get-tuple-element.14), kind=kLoop, calls=%fused_computation.17 | loop fusion | flops 6291456 | bytes 4210696 | tf_op jit(solution)/shard_map/convert_element_type | solution.py:50
  30.4 16.1 %fusion.31 = (bf16[2,1024,512]{2,1,0:T(8,128)(2,1)S(1)}, bf16[2,1024,512]{2,1,0:T(8,128)(2,1)S(1)}) fusion(f32[2,1024]{1,0:T(2,128)S(1)} %get-tuple-element.14, f32[1024,512]{1,0:T(8,128)S(1)} %multiply_add_fusion, f32[2]{0:T(128)S(1)} %add_multiply_fusion, f32[2,1024]{1,0:T(2,128)S(1)} %get-tuple-element.15), kind=kLoop, calls=%fused_computation.73 | loop fusion | flops 9437184 | bytes 6307848 | tf_op jit(solution)/shard_map/neg | solution.py:53
  46.6 3.9 %maximum_bitcast_fusion = (bf16[2,1,1024,1024]{3,2,1,0:T(8,128)(2,1)}, bf16[2,1,1024,1024]{3,2,1,0:T(8,128)(2,1)}) fusion(bf16[2,1024,512]{2,1,0:T(8,128)(2,1)S(1)} %get-tuple-element.9, bf16[2,1024,512]{2,1,0:T(8,128)(2,1)S(1)} %fusion.10, bf16[2,1024,512]{2,1,0:T(8,128)(2,1)S(1)} %get-tuple-element.8), kind=kLoop, calls=%fused_computation.21 | loop fusion | flops 16777216 | bytes 14680064 | tf_op jit(solution)/shard_map/stack | solution.py:54
  50.5 7.7 %all-to-all-done = bf16[2,256,1,8,256]{4,1,2,0,3:T(8,128)(2,1)S(1)} async-done(((bf16[2,256,1,8,256]{4,1,2,0,3:T(8,128)(2,1)}), bf16[2,256,1,8,256]{4,1,2,0,3:T(8,128)(2,1)S(1)}, u32[]{:S(2)}, u32[]{:S(2)}) %all-to-all-start) | async-done | bytes 2097184 | tf_op jit(solution)/shard_map/all_to_all | solution.py:76
  58.1 1.5 %copy.30 = bf16[2,256,1,8,256]{4,1,3,0,2:T(8,128)(2,1)} copy(bf16[2,256,1,8,256]{4,1,2,0,3:T(8,128)(2,1)S(1)} %all-to-all-done) | data formatting | bytes 4194304 | tf_op jit(solution)/shard_map/all_to_all | solution.py:76
  59.6 3.1 %copy.31 = bf16[2,4,256,1,2,256]{2,1,5,0,4,3:T(4,128)(2,1)S(1)} copy(bf16[2,4,256,1,2,256]{5,2,4,1,0,3:T(8,128)(2,1)} %bitcast.73) | data formatting | bytes 4194304 | tf_op jit(solution)/shard_map/all_to_all | solution.py:76
  62.7 2.7 %reshape.148 = bf16[2,1024,2,256]{1,3,0,2:T(8,128)(2,1)} reshape(bf16[2,4,256,1,2,256]{2,1,5,0,4,3:T(4,128)(2,1)S(1)} %copy.31) | data formatting | bytes 4194304 | tf_op jit(solution)/shard_map/reshape | solution.py:77
  65.4 5.4 %fusion.14 = f32[2,256,1024]{2,1,0:T(8,128)S(1)} fusion(bf16[2,1024,2,256]{1,3,0,2:T(8,128)(2,1)} %reshape.148, bf16[2,1,1024,1024]{3,2,1,0:T(8,128)(2,1)} %get-tuple-element.11, bf16[2,1,1024,1024]{3,2,1,0:T(8,128)(2,1)} %get-tuple-element.10), kind=kOutput, calls=%fused_computation.24 | convolution fusion | flops 2164260864 | bytes 12582912 | tf_op jit(solution)/shard_map/pacn,cpaq->cnq/dot_general | solution.py:78
  70.9 0.5 fusion.19
  71.6 1.1 %gather_fusion.1 = f32[2,32,512]{2,0,1:T(2,128)S(1)} fusion(f32[2,64,512]{2,0,1:T(2,128)S(1)} %pad_maximum_fusion, s32[2]{0:T(128)S(1)} %fusion.29), kind=kCustom, calls=%fused_computation.1 | custom fusion | bytes 262168 | tf_op jit(solution)/shard_map/vmap()/gather | solution.py:21
  73.0 4.8 %collective-permute-done = f32[2,32,512]{2,0,1:T(2,128)S(1)} collective-permute-done((f32[2,32,512]{2,0,1:T(2,128)S(1)}, f32[2,32,512]{2,0,1:T(2,128)S(1)}, u32[]{:S(2)}, u32[]{:S(2)}) %collective-permute-start) | collective-permute-done | bytes 131104 | tf_op jit(solution)/shard_map/ppermute | solution.py:13
  78.0 1.1 %gather_fusion.2 = f32[2,32,512]{2,0,1:T(2,128)S(1)} fusion(f32[2,64,512]{2,0,1:T(2,128)S(1)} %pad_maximum_fusion.1, s32[2]{0:T(128)S(1)} %fusion.28), kind=kCustom, calls=%fused_computation.2 | custom fusion | bytes 262168 | tf_op jit(solution)/shard_map/vmap()/gather | solution.py:21
  79.5 6.5 %collective-permute-done.1 = f32[2,32,512]{2,0,1:T(2,128)S(1)} collective-permute-done((f32[2,32,512]{2,0,1:T(2,128)S(1)}, f32[2,32,512]{2,0,1:T(2,128)S(1)}, u32[]{:S(2)}, u32[]{:S(2)}) %collective-permute-start.1) | collective-permute-done | bytes 131104 | tf_op jit(solution)/shard_map/ppermute | solution.py:13
  86.1 1.1 %gather_fusion.3 = f32[2,32,512]{2,0,1:T(2,128)S(1)} fusion(f32[2,64,512]{2,0,1:T(2,128)S(1)} %pad_maximum_fusion.2, s32[2]{0:T(128)S(1)} %fusion.27), kind=kCustom, calls=%fused_computation.3 | custom fusion | bytes 262168 | tf_op jit(solution)/shard_map/vmap()/gather | solution.py:21
  87.2 1.6 %collective-permute-start.2 = (f32[2,32,512]{2,0,1:T(2,128)S(1)}, f32[2,32,512]{2,0,1:T(2,128)S(1)}, u32[]{:S(2)}, u32[]{:S(2)}) collective-permute-start(f32[2,32,512]{2,0,1:T(2,128)S(1)} %bitcast.75), channel_id=1, source_target_pairs={{0,2},{2,0},{1,3},{3,1},{4,6},{6,4},{5,7},{7,5},{8,10},{10,8},{9,1... | collective-permute-start | bytes 393224 | tf_op jit(solution)/shard_map/ppermute | solution.py:13
  88.9 3.3 %collective-permute-done.2 = f32[2,32,512]{2,0,1:T(2,128)S(1)} collective-permute-done((f32[2,32,512]{2,0,1:T(2,128)S(1)}, f32[2,32,512]{2,0,1:T(2,128)S(1)}, u32[]{:S(2)}, u32[]{:S(2)}) %collective-permute-start.2) | collective-permute-done | bytes 131104 | tf_op jit(solution)/shard_map/ppermute | solution.py:13
  92.4 1.1 %gather_fusion.4 = f32[2,32,512]{2,0,1:T(2,128)S(1)} fusion(f32[2,64,512]{2,0,1:T(2,128)S(1)} %pad_maximum_fusion.3, s32[2]{0:T(128)S(1)} %fusion.26), kind=kCustom, calls=%fused_computation.4 | custom fusion | bytes 262168 | tf_op jit(solution)/shard_map/vmap()/gather | solution.py:21
  93.5 0.7 copy.32
  (43 shorter events, 1.8 us)
Async XLA Ops:
  0.0 9.9 %copy-start = (f32[3,1024]{1,0:T(4,128)S(1)}, f32[3,1024]{1,0:T(4,128)}, u32[]{:S(2)}) copy-start(f32[3,1024]{1,0:T(4,128)} %param.9) | copy-start | bytes 36868
  0.0 10.2 %copy-start.3 = (s32[4,2,8]{2,1,0:T(2,128)S(1)}, s32[4,2,8]{2,1,0:T(2,128)}, u32[]{:S(2)}) copy-start(s32[4,2,8]{2,1,0:T(2,128)} %param.13) | copy-start | bytes 772
  0.0 10.3 %copy-start.4 = (s32[1024]{0:T(1024)S(1)}, s32[1024]{0:T(1024)}, u32[]{:S(2)}) copy-start(s32[1024]{0:T(1024)} %param.11) | copy-start | bytes 12292
  0.0 13.1 %copy-start.5 = (s32[16]{0:T(128)S(1)}, s32[16]{0:T(128)}, u32[]{:S(2)}) copy-start(s32[16]{0:T(128)} %param.12) | copy-start | bytes 196
  3.5 10.6 %copy-start.2 = (f32[3,512]{1,0:T(4,128)S(1)}, f32[3,512]{1,0:T(4,128)}, u32[]{:S(2)}) copy-start(f32[3,512]{1,0:T(4,128)} %param.10) | copy-start | bytes 18436
  3.5 10.6 %copy-start.1 = (f32[2,1,2,1024]{3,2,1,0:T(2,128)S(1)}, f32[2,1,2,1024]{3,2,1,0:T(2,128)}, u32[]{:S(2)}) copy-start(f32[2,1,2,1024]{3,2,1,0:T(2,128)} %param.8) | copy-start | bytes 49156
  3.5 54.6 %all-to-all-start = ((bf16[2,256,1,8,256]{4,1,2,0,3:T(8,128)(2,1)}), bf16[2,256,1,8,256]{4,1,2,0,3:T(8,128)(2,1)S(1)}, u32[]{:S(2)}, u32[]{:S(2)}) async-start(bf16[2,256,1,8,256]{4,1,2,0,3:T(8,128)(2,1)} %copy.29), calls=%async_computation | async-start | bytes 4194304 | tf_op jit(solution)/shard_map/all_to_all | solution.py:76
  72.8 5.0 %collective-permute-start = (f32[2,32,512]{2,0,1:T(2,128)S(1)}, f32[2,32,512]{2,0,1:T(2,128)S(1)}, u32[]{:S(2)}, u32[]{:S(2)}) collective-permute-start(f32[2,32,512]{2,0,1:T(2,128)S(1)} %broadcast_add_fusion), channel_id=1, source_target_pairs={{0,4},{4,0},{8,12},{12,8},{1,5},{5,1},{9,13},{13,9},{2,6},{6,2},{1... | collective-permute-start | bytes 393224 | tf_op jit(solution)/shard_map/ppermute | solution.py:13
  79.2 6.8 %collective-permute-start.1 = (f32[2,32,512]{2,0,1:T(2,128)S(1)}, f32[2,32,512]{2,0,1:T(2,128)S(1)}, u32[]{:S(2)}, u32[]{:S(2)}) collective-permute-start(f32[2,32,512]{2,0,1:T(2,128)S(1)} %select_add_fusion.1), channel_id=1, source_target_pairs={{0,8},{4,12},{8,0},{12,4},{1,9},{5,13},{9,1},{13,5},{2,10},{6,14},... | collective-permute-start | bytes 393224 | tf_op jit(solution)/shard_map/ppermute | solution.py:13
  87.2 5.0 %collective-permute-start.2 = (f32[2,32,512]{2,0,1:T(2,128)S(1)}, f32[2,32,512]{2,0,1:T(2,128)S(1)}, u32[]{:S(2)}, u32[]{:S(2)}) collective-permute-start(f32[2,32,512]{2,0,1:T(2,128)S(1)} %bitcast.75), channel_id=1, source_target_pairs={{0,2},{2,0},{1,3},{3,1},{4,6},{6,4},{5,7},{7,5},{8,10},{10,8},{9,1... | collective-permute-start | bytes 393224 | tf_op jit(solution)/shard_map/ppermute | solution.py:13
where the time goes:
time: 94.5 us; the launch traced here: 94.2 us
  other arithmetic  38.1 us (40%)
  waiting for transfers between devices  22.3 us (24%)
  local copies, waits for them, and re-layouts  20 us (21%)
  starting transfers between devices  8.15 us (9%)
  matrix products  5.44 us (6%)
    neg x1, other arithmetic, beam_weights(): lower_rows = jnp.concatenate([-w_im, w_re], axis=2)  16.1 us
    convert_element_type x1, other arithmetic, beam_weights(): w_re = ((g_re * cosine + g_im * sine) * factor).astype(jnp.bfloat16)  15.9 us
    ppermute x3, waiting for transfers between devices, partner_2(): return lax.ppermute(value, axis, pairs)  14.6 us
    all_to_all x1, waiting for transfers between devices, shards(): lax.all_to_all(voltages, 'chan', split_axis=3, concat_axis=1, tiled=True)  7.65 us
    all_to_all x1, starting transfers between devices, shards(): lax.all_to_all(voltages, 'chan', split_axis=3, concat_axis=1, tiled=True)  6.45 us
    dot_general x1, matrix products, shards(): jnp.einsum('pacn,cpaq->cnq', flat, weights, preferred_element_type=jnp.fl...  5.44 us
    all_to_all x2, local copies, waits for them, and re-layouts, shards(): lax.all_to_all(voltages, 'chan', split_axis=3, concat_axis=1, tiled=True)  4.56 us
    gather x4, local copies, waits for them, and re-layouts, one_row(): return lax.dynamic_slice_in_dim(row, length - shift, length, 0)  4.3 us
  transfers between devices with their start and end apart: 4, of which 4 were waited for; matrix products, arithmetic and copies ran while one was open for 43% of the time, Pallas kernels for 0%

commit v1 on v0

--- a/solution.py
+++ b/solution.py
@@ -73,7 +73,10 @@
     freq = 1.0 + lax.dynamic_slice_in_dim(chan_order, base, per_dev).astype(jnp.float32) / total
     pos_rows = positions[:, antenna_row_lookup]
     weights = beam_weights(gains[:, 0], freq, pos_rows, directions)
-    turned = lax.all_to_all(voltages, "chan", split_axis=3, concat_axis=1, tiled=True)
+    turned = jnp.concatenate(
+        lax.all_to_all(jnp.stack(jnp.split(voltages, lax.axis_size("chan"), axis=3)), "chan", 0, 0),
+        axis=1,
+    )
     flat = turned.reshape(turned.shape[0], turned.shape[1], turned.shape[3], turned.shape[4])
     beams = jnp.einsum("pacn,cpaq->cnq", flat, weights, preferred_element_type=jnp.float32)
     half = beams.shape[2] // 2

time: 94.5 us -> 102 us (1.079)
  other arithmetic: 38.1 us -> 42.8 us
  local copies, waits for them, and re-layouts: 20 us -> 23.6 us
    another operation x0 -> x3, local copies, waits for them, and re-layouts: none -> 9.6 us  [the longest x2 6.37 us: shards(): jnp.stack(jnp.split(voltages, lax.axis_size('chan'), axis=3))]
    another operation x0 -> x1, other arithmetic: none -> 4.69 us  [shards(): jnp.stack(jnp.split(voltages, lax.axis_size('chan'), axis=3))]
    all_to_all x2 -> x0, local copies, waits for them, and re-layouts: 4.56 us -> none  [shards(): lax.all_to_all(voltages, 'chan', split_axis=3, concat_axis=1, tiled=True)]
    unnamed x14 -> x13, local copies, waits for them, and re-layouts: 3.71 us -> 0.25 us
    reshape x1, local copies, waits for them, and re-layouts: 2.74 us -> 4.82 us  [shards(): jnp.concatenate(lax.all_to_all(jnp.stack(jnp.split(voltages, lax.axis_siz...]
  transfers between devices with their start and end apart: 4 -> 4, of which waited for: 4 -> 4; matrix products, arithmetic and copies ran while one was open for 43% -> 40% of each run, Pallas kernels for 0% -> 0%
where the time goes in v1:
time: 102 us
  other arithmetic  42.8 us (42%)
  local copies, waits for them, and re-layouts  23.6 us (23%)
  waiting for transfers between devices  22.3 us (22%)
  starting transfers between devices  8.15 us (8%)
  matrix products  4.76 us (5%)
    neg x1, other arithmetic, beam_weights(): lower_rows = jnp.concatenate([-w_im, w_re], axis=2)  16.1 us
    convert_element_type x1, other arithmetic, beam_weights(): w_re = ((g_re * cosine + g_im * sine) * factor).astype(jnp.bfloat16)  15.9 us
    ppermute x3, waiting for transfers between devices, partner_2(): return lax.ppermute(value, axis, pairs)  14.6 us
    all_to_all x1, waiting for transfers between devices, shards(): lax.all_to_all(jnp.stack(jnp.split(voltages, lax.axis_size('chan'), axis=...  7.65 us
    all_to_all x1, starting transfers between devices, shards(): lax.all_to_all(jnp.stack(jnp.split(voltages, lax.axis_size('chan'), axis=...  6.45 us
    another operation x2, local copies, waits for them, and re-layouts, shards(): jnp.stack(jnp.split(voltages, lax.axis_size('chan'), axis=3))  6.37 us
    reshape x1, local copies, waits for them, and re-layouts, shards(): jnp.concatenate(lax.all_to_all(jnp.stack(jnp.split(voltages, lax.axis_siz...  4.82 us
    dot_general x1, matrix products, shards(): jnp.einsum('pacn,cpaq->cnq', flat, weights, preferred_element_type=jnp.fl...  4.76 us
  transfers between devices with their start and end apart: 4, of which 4 were waited for; matrix products, arithmetic and copies ran while one was open for 40% of the time, Pallas kernels for 0%

profile of v1, /device:TPU:0, one launch (start us, length us, event | category | flops | bytes accessed | tf_op | source)
XLA Modules:
  0.0 101.9 jit_solution(6555362902644605171)
XLA Ops:
  0.0 2.1 %slice_bitcast_fusion.3 = bf16[1,2,256,1,2,256]{5,4,2,1,3,0:T(2,128)(2,1)S(1)} fusion(bf16[2,256,1,8,256]{4,3,2,1,0:T(8,128)(2,1)} %param.7), kind=kLoop, calls=%fused_computation.37 | loop fusion | bytes 1048576 | tf_op jit(solution)/shard_map/stack | solution.py:77
  2.1 4.2 %slice_bitcast_fusion.2 = (bf16[1,2,256,1,2,256]{5,4,2,1,3,0:T(2,128)(2,1)S(1)}, bf16[1,2,256,1,2,256]{5,4,2,1,3,0:T(2,128)(2,1)S(1)}, bf16[1,2,256,1,2,256]{5,4,2,1,3,0:T(2,128)(2,1)S(1)}) fusion(bf16[2,256,1,8,256]{4,3,1,0,2:T(8,128)(2,1)} %bitcast.82), kind=kLoop, calls=%fused_computation.36 | loop fusion | bytes 3145728 | tf_op jit(solution)/shard_map/stack | solution.py:77
  6.4 4.7 %pad_maximum_fusion = bf16[4,2,256,1,2,256]{5,4,2,1,3,0:T(2,128)(2,1)} fusion(bf16[1,2,256,1,2,256]{5,4,2,1,3,0:T(2,128)(2,1)S(1)} %get-tuple-element.13, bf16[1,2,256,1,2,256]{5,4,2,1,3,0:T(2,128)(2,1)S(1)} %get-tuple-element.14, bf16[1,2,256,1,2,256]{5,4,2,1,3,0:T(2,128)(2,1)S(1)} %slice_bitcast_fusion.3, ...), kind=kLoop, calls=%fused_computation.23 | loop fusion | flops 3145728 | bytes 4194304 | tf_op jit(solution)/shard_map/stack | solution.py:77
  11.1 6.5 %all-to-all-start = ((bf16[4,2,256,1,2,256]{5,4,2,1,3,0:T(2,128)(2,1)}), bf16[4,2,256,1,2,256]{5,4,2,1,3,0:T(2,128)(2,1)S(1)}, u32[]{:S(2)}, u32[]{:S(2)}) async-start(bf16[4,2,256,1,2,256]{5,4,2,1,3,0:T(2,128)(2,1)} %pad_maximum_fusion), calls=%async_computation | async-start | bytes 4194304 | tf_op jit(solution)/shard_map/all_to_all | solution.py:77
  17.9 2.8 %gather_fusion = f32[1024,3]{1,0:T(8,128)S(1)} fusion(f32[3,1024]{0,1:T(8,128)S(1)} %copy.19, s32[1024]{0:T(1024)S(1)} %fusion.21), kind=kCustom, calls=%fused_computation | custom fusion | bytes 28672 | tf_op jit(solution)/shard_map/gather | solution.py:74
  20.9 0.8 slice_reduce_fusion.2
  21.7 0.5 multiply_add_fusion
  22.2 15.9 %fusion.10 = bf16[2,1024,512]{2,1,0:T(8,128)(2,1)S(1)} fusion(f32[2,1024]{1,0:T(2,128)S(1)} %get-tuple-element.18, f32[1024,512]{1,0:T(8,128)S(1)} %multiply_add_fusion, f32[2]{0:T(128)S(1)} %add_multiply_fusion, f32[2,1024]{1,0:T(2,128)S(1)} %get-tuple-element.17), kind=kLoop, calls=%fused_computation.17 | loop fusion | flops 6291456 | bytes 4210696 | tf_op jit(solution)/shard_map/convert_element_type | solution.py:50
  38.1 16.1 %fusion.31 = (bf16[2,1024,512]{2,1,0:T(8,128)(2,1)S(1)}, bf16[2,1024,512]{2,1,0:T(8,128)(2,1)S(1)}) fusion(f32[2,1024]{1,0:T(2,128)S(1)} %get-tuple-element.17, f32[1024,512]{1,0:T(8,128)S(1)} %multiply_add_fusion, f32[2]{0:T(128)S(1)} %add_multiply_fusion, f32[2,1024]{1,0:T(2,128)S(1)} %get-tuple-element.18), kind=kLoop, calls=%fused_computation.78 | loop fusion | flops 9437184 | bytes 6307848 | tf_op jit(solution)/shard_map/neg | solution.py:53
  54.2 3.9 %maximum_bitcast_fusion = (bf16[2,1,1024,1024]{3,2,1,0:T(8,128)(2,1)}, bf16[2,1,1024,1024]{3,2,1,0:T(8,128)(2,1)}) fusion(bf16[2,1024,512]{2,1,0:T(8,128)(2,1)S(1)} %get-tuple-element.9, bf16[2,1024,512]{2,1,0:T(8,128)(2,1)S(1)} %fusion.10, bf16[2,1024,512]{2,1,0:T(8,128)(2,1)S(1)} %get-tuple-element.8), kind=kLoop, calls=%fused_computation.21 | loop fusion | flops 16777216 | bytes 14680064 | tf_op jit(solution)/shard_map/stack | solution.py:54
  58.1 7.7 %all-to-all-done = bf16[4,2,256,1,2,256]{5,4,2,1,3,0:T(2,128)(2,1)S(1)} async-done(((bf16[4,2,256,1,2,256]{5,4,2,1,3,0:T(2,128)(2,1)}), bf16[4,2,256,1,2,256]{5,4,2,1,3,0:T(2,128)(2,1)S(1)}, u32[]{:S(2)}, u32[]{:S(2)}) %all-to-all-start) | async-done | bytes 2097184 | tf_op jit(solution)/shard_map/all_to_all | solution.py:77
  65.8 4.8 %copy.18 = bf16[2,4,256,1,2,256]{2,1,5,0,4,3:T(4,128)(2,1)} copy(bf16[2,4,256,1,2,256]{5,4,2,0,3,1:T(2,128)(2,1)S(1)} %bitcast.80) | data formatting | bytes 4194304 | tf_op jit(solution)/shard_map/reshape | solution.py:76
  70.6 3.2 %reshape_reshape.3 = bf16[2,1024,2,256]{1,3,0,2:T(8,128)(2,1)S(1)} reshape(bf16[2,4,256,1,2,256]{2,1,5,0,4,3:T(4,128)(2,1)} %copy.18) | data formatting | bytes 4194304 | tf_op jit(solution)/shard_map/reshape;reshape | solution.py:80
  73.8 4.8 %fusion.14 = f32[2,256,1024]{2,1,0:T(8,128)S(1)} fusion(bf16[2,1024,2,256]{1,3,0,2:T(8,128)(2,1)S(1)} %reshape_reshape.3, bf16[2,1,1024,1024]{3,2,1,0:T(8,128)(2,1)} %get-tuple-element.11, bf16[2,1,1024,1024]{3,2,1,0:T(8,128)(2,1)} %get-tuple-element.10), kind=kOutput, calls=%fused_computation.25 | convolution fusion | flops 2151677952 | bytes 12582912 | tf_op jit(solution)/shard_map/pacn,cpaq->cnq/dot_general | solution.py:81
  78.6 0.5 fusion.19
  79.3 1.1 %gather_fusion.1 = f32[2,32,512]{2,0,1:T(2,128)S(1)} fusion(f32[2,64,512]{2,0,1:T(2,128)S(1)} %pad_maximum_fusion.1, s32[2]{0:T(128)S(1)} %fusion.29), kind=kCustom, calls=%fused_computation.1 | custom fusion | bytes 262168 | tf_op jit(solution)/shard_map/vmap()/gather | solution.py:21
  80.7 4.8 %collective-permute-done = f32[2,32,512]{2,0,1:T(2,128)S(1)} collective-permute-done((f32[2,32,512]{2,0,1:T(2,128)S(1)}, f32[2,32,512]{2,0,1:T(2,128)S(1)}, u32[]{:S(2)}, u32[]{:S(2)}) %collective-permute-start) | collective-permute-done | bytes 131104 | tf_op jit(solution)/shard_map/ppermute | solution.py:13
  85.7 1.1 %gather_fusion.2 = f32[2,32,512]{2,0,1:T(2,128)S(1)} fusion(f32[2,64,512]{2,0,1:T(2,128)S(1)} %pad_maximum_fusion.2, s32[2]{0:T(128)S(1)} %fusion.28), kind=kCustom, calls=%fused_computation.2 | custom fusion | bytes 262168 | tf_op jit(solution)/shard_map/vmap()/gather | solution.py:21
  87.2 6.5 %collective-permute-done.1 = f32[2,32,512]{2,0,1:T(2,128)S(1)} collective-permute-done((f32[2,32,512]{2,0,1:T(2,128)S(1)}, f32[2,32,512]{2,0,1:T(2,128)S(1)}, u32[]{:S(2)}, u32[]{:S(2)}) %collective-permute-start.1) | collective-permute-done | bytes 131104 | tf_op jit(solution)/shard_map/ppermute | solution.py:13
  93.8 1.1 %gather_fusion.3 = f32[2,32,512]{2,0,1:T(2,128)S(1)} fusion(f32[2,64,512]{2,0,1:T(2,128)S(1)} %pad_maximum_fusion.3, s32[2]{0:T(128)S(1)} %fusion.27), kind=kCustom, calls=%fused_computation.3 | custom fusion | bytes 262168 | tf_op jit(solution)/shard_map/vmap()/gather | solution.py:21
  94.9 1.6 %collective-permute-start.2 = (f32[2,32,512]{2,0,1:T(2,128)S(1)}, f32[2,32,512]{2,0,1:T(2,128)S(1)}, u32[]{:S(2)}, u32[]{:S(2)}) collective-permute-start(f32[2,32,512]{2,0,1:T(2,128)S(1)} %bitcast.83), channel_id=1, source_target_pairs={{0,2},{2,0},{1,3},{3,1},{4,6},{6,4},{5,7},{7,5},{8,10},{10,8},{9,1... | collective-permute-start | bytes 393224 | tf_op jit(solution)/shard_map/ppermute | solution.py:13
  96.7 3.3 %collective-permute-done.2 = f32[2,32,512]{2,0,1:T(2,128)S(1)} collective-permute-done((f32[2,32,512]{2,0,1:T(2,128)S(1)}, f32[2,32,512]{2,0,1:T(2,128)S(1)}, u32[]{:S(2)}, u32[]{:S(2)}) %collective-permute-start.2) | collective-permute-done | bytes 131104 | tf_op jit(solution)/shard_map/ppermute | solution.py:13
  100.1 1.1 %gather_fusion.4 = f32[2,32,512]{2,0,1:T(2,128)S(1)} fusion(f32[2,64,512]{2,0,1:T(2,128)S(1)} %pad_maximum_fusion.4, s32[2]{0:T(128)S(1)} %fusion.26), kind=kCustom, calls=%fused_computation.4 | custom fusion | bytes 262168 | tf_op jit(solution)/shard_map/vmap()/gather | solution.py:21
  101.3 0.7 copy.21
  (44 shorter events, 2.0 us)
Async XLA Ops:
  6.4 11.2 %copy-start = (f32[3,1024]{1,0:T(4,128)S(1)}, f32[3,1024]{1,0:T(4,128)}, u32[]{:S(2)}) copy-start(f32[3,1024]{1,0:T(4,128)} %param.9) | copy-start | bytes 36868
  6.4 11.4 %copy-start.3 = (s32[4,2,8]{2,1,0:T(2,128)S(1)}, s32[4,2,8]{2,1,0:T(2,128)}, u32[]{:S(2)}) copy-start(s32[4,2,8]{2,1,0:T(2,128)} %param.13) | copy-start | bytes 772
  6.4 11.5 %copy-start.4 = (s32[1024]{0:T(1024)S(1)}, s32[1024]{0:T(1024)}, u32[]{:S(2)}) copy-start(s32[1024]{0:T(1024)} %param.11) | copy-start | bytes 12292
  6.4 14.3 %copy-start.5 = (s32[16]{0:T(128)S(1)}, s32[16]{0:T(128)}, u32[]{:S(2)}) copy-start(s32[16]{0:T(128)} %param.12) | copy-start | bytes 196
  11.1 10.6 %copy-start.2 = (f32[3,512]{1,0:T(4,128)S(1)}, f32[3,512]{1,0:T(4,128)}, u32[]{:S(2)}) copy-start(f32[3,512]{1,0:T(4,128)} %param.10) | copy-start | bytes 18436
  11.1 10.6 %copy-start.1 = (f32[2,1,2,1024]{3,2,1,0:T(2,128)S(1)}, f32[2,1,2,1024]{3,2,1,0:T(2,128)}, u32[]{:S(2)}) copy-start(f32[2,1,2,1024]{3,2,1,0:T(2,128)} %param.8) | copy-start | bytes 49156
  11.1 54.6 %all-to-all-start = ((bf16[4,2,256,1,2,256]{5,4,2,1,3,0:T(2,128)(2,1)}), bf16[4,2,256,1,2,256]{5,4,2,1,3,0:T(2,128)(2,1)S(1)}, u32[]{:S(2)}, u32[]{:S(2)}) async-start(bf16[4,2,256,1,2,256]{5,4,2,1,3,0:T(2,128)(2,1)} %pad_maximum_fusion), calls=%async_computation | async-start | bytes 4194304 | tf_op jit(solution)/shard_map/all_to_all | solution.py:77
  80.5 5.0 %collective-permute-start = (f32[2,32,512]{2,0,1:T(2,128)S(1)}, f32[2,32,512]{2,0,1:T(2,128)S(1)}, u32[]{:S(2)}, u32[]{:S(2)}) collective-permute-start(f32[2,32,512]{2,0,1:T(2,128)S(1)} %broadcast_add_fusion), channel_id=1, source_target_pairs={{0,4},{4,0},{8,12},{12,8},{1,5},{5,1},{9,13},{13,9},{2,6},{6,2},{1... | collective-permute-start | bytes 393224 | tf_op jit(solution)/shard_map/ppermute | solution.py:13
  86.9 6.8 %collective-permute-start.1 = (f32[2,32,512]{2,0,1:T(2,128)S(1)}, f32[2,32,512]{2,0,1:T(2,128)S(1)}, u32[]{:S(2)}, u32[]{:S(2)}) collective-permute-start(f32[2,32,512]{2,0,1:T(2,128)S(1)} %select_add_fusion.1), channel_id=1, source_target_pairs={{0,8},{4,12},{8,0},{12,4},{1,9},{5,13},{9,1},{13,5},{2,10},{6,14},... | collective-permute-start | bytes 393224 | tf_op jit(solution)/shard_map/ppermute | solution.py:13
  94.9 5.0 %collective-permute-start.2 = (f32[2,32,512]{2,0,1:T(2,128)S(1)}, f32[2,32,512]{2,0,1:T(2,128)S(1)}, u32[]{:S(2)}, u32[]{:S(2)}) collective-permute-start(f32[2,32,512]{2,0,1:T(2,128)S(1)} %bitcast.83), channel_id=1, source_target_pairs={{0,2},{2,0},{1,3},{3,1},{4,6},{6,4},{5,7},{7,5},{8,10},{10,8},{9,1... | collective-permute-start | bytes 393224 | tf_op jit(solution)/shard_map/ppermute | solution.py:13
